TPU v7x, 128 devices: a whole 4x4x4 slice. The times are simulated.
128 devices in a mesh: inner: 16 (over x_lo, z, core), outer: 8 (over x_hi, y).
Axes of the slice: x: 4 (x_hi: 2, x_lo: 2; x = x_hi * 2 + x_lo), y: 4, z: 4, core: 2. Of those that a mesh axis runs over, the one named last changes fastest.
Arguments:
- layer_input: bfloat16 [16384, 6144], P(('inner', 'outer')), may hold values from -0.25 to 0.25
- queries: bfloat16 [16384, 768], P(('inner', 'outer')), may hold values from -6 to 6
- keys_values: bfloat16 [16384, 256], P(('inner', 'outer')), may hold values from -6 to 6
- attn_out: bfloat16 [16384, 768], P(('inner', 'outer')), may hold values from -6 to 6
- out_grad: bfloat16 [16384, 768], P(('inner', 'outer')), may hold values from -6 to 6
- log_sums: float32 [6, 16384], P(None, ('inner', 'outer')), may hold values from 5 to 8
- doc_ids: int32 [16384], replicated, may hold values from 0 to 15, never falling along the last dimension, each value on 1 to 2048 neighbouring positions
- span_order: int32 [256], replicated, may hold values from 0 to 255, each once
Outputs:
- query_grad: bfloat16 [16384, 768], P(('inner', 'outer'))
- kv_grad: bfloat16 [16384, 256], P(('inner', 'outer'))
- weight_grad: float32 [6144, 256], P(('inner', 'outer'))
Inputs may be any that keep to these rules, and one draw needn't show every extreme that they name: `doc_ids`: never falling; each document holds 1 to 2048 positions. `span_order`: each span number once.
All inputs are finite; a program needn't handle non-finite values.
Results may differ from a plain program's by a relative error of at most 0.015.
Values may be sent and summed in bfloat16 or wider, within the bound.
A program may use at most 64 MiB of HBM per device.

v0:
```python
import jax
import jax.numpy as jnp
from jax import lax
from jax.sharding import PartitionSpec as P


def passed_along(value, axis, by):
    devices = lax.axis_size(axis)
    return lax.ppermute(value, axis, [(i, (i + by) % devices) for i in range(devices)])


def per_device(
    layer_input, queries, keys_values, attn_out, out_grad, log_sums, doc_ids, span_order
):
    tok_rows = keys_values.shape[0]
    half_len = tok_rows // 2
    head_count = log_sums.shape[0]
    head_dim = keys_values.shape[1] // 2
    inner_size = lax.axis_size("inner")
    outer_size = lax.axis_size("outer")
    my_index = lax.axis_index(("inner", "outer"))
    score_scale = head_dim ** (-0.5)
    row_ids = jnp.arange(tok_rows, dtype=jnp.int32)
    my_spans = lax.dynamic_slice_in_dim(span_order, 2 * my_index, 2)
    query_pos = (
        jnp.where(row_ids < half_len, my_spans[0], my_spans[1]) * half_len + row_ids % half_len
    )
    query_doc = jnp.take(doc_ids, query_pos)
    query_heads = queries.reshape(tok_rows, head_count, head_dim)
    grad_heads = out_grad.reshape(tok_rows, head_count, head_dim)
    out_heads = attn_out.reshape(tok_rows, head_count, head_dim)
    row_delta = jnp.einsum("ihc,ihc->hi", grad_heads, out_heads, preferred_element_type=jnp.float32)

    def key_meta(base_dev, stride, group_devs):
        key_ids = jnp.arange(group_devs * tok_rows, dtype=jnp.int32)
        owner = base_dev + key_ids // tok_rows * stride
        span_ids = 2 * owner + key_ids % tok_rows // half_len
        key_pos = jnp.take(span_order, span_ids) * half_len + key_ids % half_len
        return (key_pos, jnp.take(doc_ids, key_pos))

    def sweep(key_group, kv_grads, query_acc, key_pos, key_doc):
        group_len = key_group.shape[0]
        block_len = 512

        def one_block(block_idx, state):
            first = block_idx * block_len
            key_blk = lax.dynamic_slice_in_dim(key_group, first, block_len, 0)
            pos_blk = lax.dynamic_slice_in_dim(key_pos, first, block_len, 0)
            doc_blk = lax.dynamic_slice_in_dim(key_doc, first, block_len, 0)
            allowed = (pos_blk[None, :] <= query_pos[:, None]) & (
                doc_blk[None, :] == query_doc[:, None]
            )
            grads_now, query_now = state
            key_rows = key_blk[:, :head_dim]
            value_rows = key_blk[:, head_dim:]
            scores = (
                jnp.einsum("ihc,jc->hij", query_heads, key_rows, preferred_element_type=jnp.float32)
                * score_scale
            )
            probs = jnp.exp(jnp.where(allowed[None], scores - log_sums[:, :, None], -1e30))
            probs_low = probs.astype(jnp.bfloat16)
            prob_grads = jnp.einsum(
                "ihc,jc->hij", grad_heads, value_rows, preferred_element_type=jnp.float32
            )
            score_grads = (score_scale * probs * (prob_grads - row_delta[:, :, None])).astype(
                jnp.bfloat16
            )
            query_now = query_now + jnp.einsum(
                "hij,jc->ihc", score_grads, key_rows, preferred_element_type=jnp.float32
            )
            key_part = jnp.einsum(
                "hij,ihc->jc", score_grads, query_heads, preferred_element_type=jnp.float32
            )
            value_part = jnp.einsum(
                "hij,ihc->jc", probs_low, grad_heads, preferred_element_type=jnp.float32
            )
            updated = lax.dynamic_slice_in_dim(grads_now, first, block_len, 0) + jnp.concatenate(
                [key_part, value_part], axis=1
            )
            grads_now = lax.dynamic_update_slice_in_dim(grads_now, updated, first, 0)
            return (grads_now, query_now)

        return lax.fori_loop(0, group_len // block_len, one_block, (kv_grads, query_acc))

    query_zero = jnp.zeros((tok_rows, head_count, head_dim), jnp.float32)
    key_group = lax.all_gather(keys_values, "outer", axis=0, tiled=True)
    inner_pos = lax.axis_index("inner")

    def hop_inner(hop_idx, state):
        group_now, grads_now, query_now = state
        source = (inner_pos - hop_idx) % inner_size
        key_pos, key_doc = key_meta(source * outer_size, 1, outer_size)
        grads_now, query_now = sweep(group_now, grads_now, query_now, key_pos, key_doc)
        grads_now = passed_along(grads_now.astype(jnp.bfloat16), "inner", 1).astype(grads_now.dtype)
        group_now = passed_along(group_now, "inner", 1)
        return (group_now, grads_now, query_now)

    start = (key_group, jnp.zeros((key_group.shape[0], 2 * head_dim), jnp.float32), query_zero)
    key_group, kv_grads, query_acc = lax.fori_loop(0, inner_size, hop_inner, start)
    kv_total = lax.psum_scatter(
        kv_grads.astype(jnp.bfloat16), "outer", scatter_dimension=0, tiled=True
    )
    query_grad = query_acc.astype(jnp.bfloat16).reshape(tok_rows, head_count * head_dim)
    weight_grad = lax.psum_scatter(
        lax.dot_general(
            layer_input, kv_total, (((0,), (0,)), ((), ())), preferred_element_type=jnp.float32
        ),
        ("inner", "outer"),
        scatter_dimension=0,
        tiled=True,
    )
    return (query_grad, kv_total, weight_grad)


def solution(mesh):
    return jax.shard_map(
        per_device,
        mesh=mesh,
        in_specs=(
            P(("inner", "outer"), None),
            P(("inner", "outer"), None),
            P(("inner", "outer"), None),
            P(("inner", "outer"), None),
            P(("inner", "outer"), None),
            P(None, ("inner", "outer")),
            P(),
            P(),
        ),
        out_specs=(
            P(("inner", "outer"), None),
            P(("inner", "outer"), None),
            P(("inner", "outer"), None),
        ),
        check_vma=False,
    )
```

profile of v0, /device:TPU:0, one launch (start us, length us, event | category | flops | bytes accessed | tf_op | source)
XLA Modules:
  0.0 1487.1 jit_solution(5365712212598533073)
XLA Ops:
  16.5 35.7 %all_gather.3 = bf16[1024,256]{1,0:T(8,128)(2,1)S(1)} all-gather(bf16[128,256]{1,0:T(8,128)(2,1)S(1)} %copy-done.4), channel_id=1, replica_groups=mesh['inner'=16,'outer'=8] {'outer'}, dimensions={0}, use_global_device_ids=true | all-gather | bytes 589824 | tf_op jit(solution)/shard_map/all_gather | solution.py:86
  52.4 691.4 %while.64 = (s32[]{:T(128)}, bf16[1024,256]{1,0:T(8,128)(2,1)S(1)}, f32[1024,256]{0,1:T(8,128)}, f32[128,6,128]{0,2,1:T(8,128)S(1)}, s32[]{:T(128)}, /*index=5*/...) while((s32[]{:T(128)}, bf16[1024,256]{1,0:T(8,128)(2,1)S(1)}, ...), condition=%wide.region_3.4_spmd.clone, body=%wide.region_0.3_spmd.clone.sunk | while | flops 507945216 | bytes 26042736 | solution.py:99
  52.5 6.9 gather_fusion
  59.4 6.2 gather_fusion.1
  67.8 10.4 while.65
  81.1 8.9 collective-permute-done.1
  95.7 6.9 gather_fusion
  102.6 6.2 gather_fusion.1
  111.0 10.4 while.65
  122.3 10.9 collective-permute-done.1
  138.9 6.9 gather_fusion
  145.8 6.2 gather_fusion.1
  154.3 10.4 while.65
  165.5 10.9 collective-permute-done.1
  182.1 6.9 gather_fusion
  189.0 6.2 gather_fusion.1
  197.5 10.4 while.65
  208.7 10.9 collective-permute-done.1
  225.3 6.9 gather_fusion
  240.7 10.4 while.65
  251.9 10.9 collective-permute-done.1
  268.5 6.9 gather_fusion
  283.9 10.4 while.65
  295.1 10.9 collective-permute-done.1
  311.7 6.9 gather_fusion
  318.6 6.2 gather_fusion.1
  327.1 10.4 while.65
  338.3 10.9 collective-permute-done.1
  354.9 6.9 gather_fusion
  361.9 6.2 gather_fusion.1
  370.3 10.4 while.65
  381.6 10.9 collective-permute-done.1
  398.1 6.9 gather_fusion
  405.1 6.2 gather_fusion.1
  413.5 10.4 while.65
  424.8 10.9 collective-permute-done.1
  441.3 6.9 gather_fusion
  448.3 6.2 gather_fusion.1
  456.7 10.4 while.65
  468.0 10.9 collective-permute-done.1
  484.6 6.9 gather_fusion
  491.5 6.2 gather_fusion.1
  499.9 10.4 while.65
  511.2 10.9 collective-permute-done.1
  527.8 6.9 gather_fusion
  534.7 6.2 gather_fusion.1
  543.1 10.4 while.65
  554.4 10.9 collective-permute-done.1
  571.0 6.9 gather_fusion
  577.9 6.2 gather_fusion.1
  586.3 10.4 while.65
  597.6 10.9 collective-permute-done.1
  614.2 6.9 gather_fusion
  629.5 10.4 while.65
  640.8 10.9 collective-permute-done.1
  657.4 6.9 gather_fusion
  672.8 10.4 while.65
  684.0 10.9 collective-permute-done.1
  700.6 6.9 gather_fusion
  716.0 10.4 while.65
  727.2 10.9 collective-permute-done.1
  746.1 69.1 %reduce-scatter.5.cloned.1.call-done = bf16[128,256]{1,0:T(8,128)(2,1)} async-done(((bf16[1024,256]{1,0:T(8,128)(2,1)}), bf16[128,256]{1,0:T(8,128)(2,1)}) %reduce-scatter.5.cloned.1.call-update) | async-done | bytes 65552 | tf_op jit(solution)/shard_map/reduce_scatter | solution.py:100
  819.7 6.6 copy.62
  827.1 653.1 %reduce-scatter.7.cloned.1.call-done = f32[48,256]{1,0:T(8,128)} async-done(((f32[6144,256]{1,0:T(8,128)}), f32[48,256]{1,0:T(8,128)}) %reduce-scatter.7.cloned.1.call-update) | async-done | bytes 49168
  (563 shorter events, 354.5 us)
Async XLA Ops:
  7.2 808.0 %copy-start = (bf16[128,6144]{1,0:T(8,128)(2,1)S(1)}, bf16[128,6144]{1,0:T(8,128)(2,1)}, u32[]{:S(2)}) copy-start(bf16[128,6144]{1,0:T(8,128)(2,1)} %param.12) | copy-start | bytes 4718596
  7.2 45.2 %copy-start.1 = (s32[256]{0:T(256)S(1)}, s32[256]{0:T(256)}, u32[]{:S(2)}) copy-start(s32[256]{0:T(256)} %param.19) | copy-start | bytes 3076
  7.2 45.2 %copy-start.2 = (s32[16384]{0:T(1024)S(1)}, s32[16384]{0:T(1024)}, u32[]{:S(2)}) copy-start(s32[16384]{0:T(1024)} %param.18) | copy-start | bytes 196612
  7.2 9.3 copy-start.4
  7.2 45.2 %copy-start.5 = (f32[6,128]{1,0:T(8,128)S(1)}, f32[6,128]{1,0:T(8,128)}, u32[]{:S(2)}) copy-start(f32[6,128]{1,0:T(8,128)} %param.17) | copy-start | bytes 9220
  7.2 807.9 %reduce-scatter.5.cloned.1.call-start = ((), (), s32[]{:S(2)}) async-start(), calls=%async_computation.2 | async-start | bytes 589824 | tf_op jit(solution)/shard_map/reduce_scatter | solution.py:100
  65.6 2.2 copy-start.3
  79.1 10.9 collective-permute-start.1
  79.1 16.5 %collective-permute-start = (bf16[1024,256]{1,0:T(8,128)(2,1)}, bf16[1024,256]{1,0:T(8,128)(2,1)S(1)}, u32[]{:S(2)}, u32[]{:S(2)}) collective-permute-start(bf16[1024,256]{1,0:T(8,128)(2,1)} %copy.80), channel_id=1, source_target_pairs={{0,8},{8,16},{16,24},{24,32},{32,40},{40,48},{48,56},{56,64},{64,7... | collective-permute-start | bytes 1572872 | tf_op jit(solution)/shard_map/while/body/eval_jaxpr/ppermute | solution.py:9
  108.8 2.2 copy-start.3
  122.3 10.9 collective-permute-start.1
  122.3 16.5 %collective-permute-start = (bf16[1024,256]{1,0:T(8,128)(2,1)}, bf16[1024,256]{1,0:T(8,128)(2,1)S(1)}, u32[]{:S(2)}, u32[]{:S(2)}) collective-permute-start(bf16[1024,256]{1,0:T(8,128)(2,1)} %copy.80), channel_id=1, source_target_pairs={{0,8},{8,16},{16,24},{24,32},{32,40},{40,48},{48,56},{56,64},{64,7... | collective-permute-start | bytes 1572872 | tf_op jit(solution)/shard_map/while/body/eval_jaxpr/ppermute | solution.py:9
  152.0 2.2 copy-start.3
  165.5 10.9 collective-permute-start.1
  165.5 16.5 %collective-permute-start = (bf16[1024,256]{1,0:T(8,128)(2,1)}, bf16[1024,256]{1,0:T(8,128)(2,1)S(1)}, u32[]{:S(2)}, u32[]{:S(2)}) collective-permute-start(bf16[1024,256]{1,0:T(8,128)(2,1)} %copy.80), channel_id=1, source_target_pairs={{0,8},{8,16},{16,24},{24,32},{32,40},{40,48},{48,56},{56,64},{64,7... | collective-permute-start | bytes 1572872 | tf_op jit(solution)/shard_map/while/body/eval_jaxpr/ppermute | solution.py:9
  195.2 2.2 copy-start.3
  208.7 10.9 collective-permute-start.1
  208.7 16.5 %collective-permute-start = (bf16[1024,256]{1,0:T(8,128)(2,1)}, bf16[1024,256]{1,0:T(8,128)(2,1)S(1)}, u32[]{:S(2)}, u32[]{:S(2)}) collective-permute-start(bf16[1024,256]{1,0:T(8,128)(2,1)} %copy.80), channel_id=1, source_target_pairs={{0,8},{8,16},{16,24},{24,32},{32,40},{40,48},{48,56},{56,64},{64,7... | collective-permute-start | bytes 1572872 | tf_op jit(solution)/shard_map/while/body/eval_jaxpr/ppermute | solution.py:9
  238.4 2.2 copy-start.3
  251.9 10.9 collective-permute-start.1
  251.9 16.5 %collective-permute-start = (bf16[1024,256]{1,0:T(8,128)(2,1)}, bf16[1024,256]{1,0:T(8,128)(2,1)S(1)}, u32[]{:S(2)}, u32[]{:S(2)}) collective-permute-start(bf16[1024,256]{1,0:T(8,128)(2,1)} %copy.80), channel_id=1, source_target_pairs={{0,8},{8,16},{16,24},{24,32},{32,40},{40,48},{48,56},{56,64},{64,7... | collective-permute-start | bytes 1572872 | tf_op jit(solution)/shard_map/while/body/eval_jaxpr/ppermute | solution.py:9
  281.6 2.2 copy-start.3
  295.1 10.9 collective-permute-start.1
  295.1 16.5 %collective-permute-start = (bf16[1024,256]{1,0:T(8,128)(2,1)}, bf16[1024,256]{1,0:T(8,128)(2,1)S(1)}, u32[]{:S(2)}, u32[]{:S(2)}) collective-permute-start(bf16[1024,256]{1,0:T(8,128)(2,1)} %copy.80), channel_id=1, source_target_pairs={{0,8},{8,16},{16,24},{24,32},{32,40},{40,48},{48,56},{56,64},{64,7... | collective-permute-start | bytes 1572872 | tf_op jit(solution)/shard_map/while/body/eval_jaxpr/ppermute | solution.py:9
  324.8 2.2 copy-start.3
  338.3 10.9 collective-permute-start.1
  338.3 16.5 %collective-permute-start = (bf16[1024,256]{1,0:T(8,128)(2,1)}, bf16[1024,256]{1,0:T(8,128)(2,1)S(1)}, u32[]{:S(2)}, u32[]{:S(2)}) collective-permute-start(bf16[1024,256]{1,0:T(8,128)(2,1)} %copy.80), channel_id=1, source_target_pairs={{0,8},{8,16},{16,24},{24,32},{32,40},{40,48},{48,56},{56,64},{64,7... | collective-permute-start | bytes 1572872 | tf_op jit(solution)/shard_map/while/body/eval_jaxpr/ppermute | solution.py:9
  368.0 2.2 copy-start.3
  381.5 10.9 collective-permute-start.1
  381.6 16.5 %collective-permute-start = (bf16[1024,256]{1,0:T(8,128)(2,1)}, bf16[1024,256]{1,0:T(8,128)(2,1)S(1)}, u32[]{:S(2)}, u32[]{:S(2)}) collective-permute-start(bf16[1024,256]{1,0:T(8,128)(2,1)} %copy.80), channel_id=1, source_target_pairs={{0,8},{8,16},{16,24},{24,32},{32,40},{40,48},{48,56},{56,64},{64,7... | collective-permute-start | bytes 1572872 | tf_op jit(solution)/shard_map/while/body/eval_jaxpr/ppermute | solution.py:9
  411.2 2.2 copy-start.3
  424.8 10.9 collective-permute-start.1
  424.8 16.5 %collective-permute-start = (bf16[1024,256]{1,0:T(8,128)(2,1)}, bf16[1024,256]{1,0:T(8,128)(2,1)S(1)}, u32[]{:S(2)}, u32[]{:S(2)}) collective-permute-start(bf16[1024,256]{1,0:T(8,128)(2,1)} %copy.80), channel_id=1, source_target_pairs={{0,8},{8,16},{16,24},{24,32},{32,40},{40,48},{48,56},{56,64},{64,7... | collective-permute-start | bytes 1572872 | tf_op jit(solution)/shard_map/while/body/eval_jaxpr/ppermute | solution.py:9
  454.4 2.2 copy-start.3
  468.0 10.9 collective-permute-start.1
  468.0 16.5 %collective-permute-start = (bf16[1024,256]{1,0:T(8,128)(2,1)}, bf16[1024,256]{1,0:T(8,128)(2,1)S(1)}, u32[]{:S(2)}, u32[]{:S(2)}) collective-permute-start(bf16[1024,256]{1,0:T(8,128)(2,1)} %copy.80), channel_id=1, source_target_pairs={{0,8},{8,16},{16,24},{24,32},{32,40},{40,48},{48,56},{56,64},{64,7... | collective-permute-start | bytes 1572872 | tf_op jit(solution)/shard_map/while/body/eval_jaxpr/ppermute | solution.py:9
  497.6 2.2 copy-start.3
  511.2 10.9 collective-permute-start.1
  511.2 16.5 %collective-permute-start = (bf16[1024,256]{1,0:T(8,128)(2,1)}, bf16[1024,256]{1,0:T(8,128)(2,1)S(1)}, u32[]{:S(2)}, u32[]{:S(2)}) collective-permute-start(bf16[1024,256]{1,0:T(8,128)(2,1)} %copy.80), channel_id=1, source_target_pairs={{0,8},{8,16},{16,24},{24,32},{32,40},{40,48},{48,56},{56,64},{64,7... | collective-permute-start | bytes 1572872 | tf_op jit(solution)/shard_map/while/body/eval_jaxpr/ppermute | solution.py:9
  540.8 2.2 copy-start.3
  554.4 10.9 collective-permute-start.1
  554.4 16.5 %collective-permute-start = (bf16[1024,256]{1,0:T(8,128)(2,1)}, bf16[1024,256]{1,0:T(8,128)(2,1)S(1)}, u32[]{:S(2)}, u32[]{:S(2)}) collective-permute-start(bf16[1024,256]{1,0:T(8,128)(2,1)} %copy.80), channel_id=1, source_target_pairs={{0,8},{8,16},{16,24},{24,32},{32,40},{40,48},{48,56},{56,64},{64,7... | collective-permute-start | bytes 1572872 | tf_op jit(solution)/shard_map/while/body/eval_jaxpr/ppermute | solution.py:9
  584.1 2.2 copy-start.3
  597.6 10.9 collective-permute-start.1
  597.6 16.5 %collective-permute-start = (bf16[1024,256]{1,0:T(8,128)(2,1)}, bf16[1024,256]{1,0:T(8,128)(2,1)S(1)}, u32[]{:S(2)}, u32[]{:S(2)}) collective-permute-start(bf16[1024,256]{1,0:T(8,128)(2,1)} %copy.80), channel_id=1, source_target_pairs={{0,8},{8,16},{16,24},{24,32},{32,40},{40,48},{48,56},{56,64},{64,7... | collective-permute-start | bytes 1572872 | tf_op jit(solution)/shard_map/while/body/eval_jaxpr/ppermute | solution.py:9
  627.3 2.2 copy-start.3
  640.8 10.9 collective-permute-start.1
  640.8 16.5 %collective-permute-start = (bf16[1024,256]{1,0:T(8,128)(2,1)}, bf16[1024,256]{1,0:T(8,128)(2,1)S(1)}, u32[]{:S(2)}, u32[]{:S(2)}) collective-permute-start(bf16[1024,256]{1,0:T(8,128)(2,1)} %copy.80), channel_id=1, source_target_pairs={{0,8},{8,16},{16,24},{24,32},{32,40},{40,48},{48,56},{56,64},{64,7... | collective-permute-start | bytes 1572872 | tf_op jit(solution)/shard_map/while/body/eval_jaxpr/ppermute | solution.py:9
  670.5 2.2 copy-start.3
  684.0 10.9 collective-permute-start.1
  684.0 16.5 %collective-permute-start = (bf16[1024,256]{1,0:T(8,128)(2,1)}, bf16[1024,256]{1,0:T(8,128)(2,1)S(1)}, u32[]{:S(2)}, u32[]{:S(2)}) collective-permute-start(bf16[1024,256]{1,0:T(8,128)(2,1)} %copy.80), channel_id=1, source_target_pairs={{0,8},{8,16},{16,24},{24,32},{32,40},{40,48},{48,56},{56,64},{64,7... | collective-permute-start | bytes 1572872 | tf_op jit(solution)/shard_map/while/body/eval_jaxpr/ppermute | solution.py:9
  713.7 2.2 copy-start.3
  727.2 10.9 collective-permute-start.1
  727.2 16.5 %collective-permute-start = (bf16[1024,256]{1,0:T(8,128)(2,1)}, bf16[1024,256]{1,0:T(8,128)(2,1)S(1)}, u32[]{:S(2)}, u32[]{:S(2)}) collective-permute-start(bf16[1024,256]{1,0:T(8,128)(2,1)} %copy.80), channel_id=1, source_target_pairs={{0,8},{8,16},{16,24},{24,32},{32,40},{40,48},{48,56},{56,64},{64,7... | collective-permute-start | bytes 1572872 | tf_op jit(solution)/shard_map/while/body/eval_jaxpr/ppermute | solution.py:9
  746.0 734.2 %reduce-scatter.7.cloned.1.call-start = ((), (), s32[]{:S(2)}) async-start(), calls=%async_computation.3 | async-start | bytes 6340608
Sparse Core Ops, SparseCore 0:
  746.2 68.9 reduce-scatter.4
  826.4 653.8 reduce-scatter.6
where the time goes:
time: 1490 us
  waiting for transfers between devices  968 us (65%)
  local copies, waits for them, and re-layouts  243 us (16%)
  matrix products  153 us (10%)
  other arithmetic  68.1 us (5%)
  blocking collectives  35.7 us (2%)
    unnamed x3, waiting for transfers between devices  653 us
    ppermute x32, waiting for transfers between devices, passed_along(): lax.ppermute(value, axis, [(i, (i + by) % devices) for i in range(devices)])  245 us
    gather x16, local copies, waits for them, and re-layouts, key_meta(): key_pos = jnp.take(span_order, span_ids) * half_len + key_ids % half_len  110 us
    gather x16, local copies, waits for them, and re-layouts, key_meta(): return (key_pos, jnp.take(doc_ids, key_pos))  98.5 us
    reduce_scatter x1, waiting for transfers between devices, per_device(): lax.psum_scatter(kv_grads.astype(jnp.bfloat16), 'outer', scatter_dimensio...  69.1 us
    dot_general x32, matrix products, one_block(): jnp.einsum('ihc,jc->hij', query_heads, key_rows, preferred_element_type=j...  43.8 us
    dot_general x32, matrix products, one_block(): jnp.einsum('ihc,jc->hij', grad_heads, value_rows, preferred_element_type=...  41 us
    dot_general x32, matrix products, one_block(): jnp.einsum('hij,jc->ihc', score_grads, key_rows, preferred_element_type=j...  39 us
  transfers between devices with their start and end apart: 34, of which 34 were waited for; matrix products, arithmetic and copies ran while one was open for 1% of the time, Pallas kernels for 0%

commit v1 on v0

--- a/solution.py
+++ b/solution.py
@@ -83,7 +83,15 @@
         return lax.fori_loop(0, group_len // block_len, one_block, (kv_grads, query_acc))
 
     query_zero = jnp.zeros((tok_rows, head_count, head_dim), jnp.float32)
-    key_group = lax.all_gather(keys_values, "outer", axis=0, tiled=True)
+    key_group = jnp.concatenate(
+        jax.lax.all_to_all(
+            jnp.stack([keys_values] * jax.lax.axis_size("outer")),
+            axis_name="outer",
+            split_axis=0,
+            concat_axis=0,
+        ),
+        axis=0,
+    )
     inner_pos = lax.axis_index("inner")
 
     def hop_inner(hop_idx, state):

time: 1490 us -> 1460 us (0.980)
  blocking collectives: 35.7 us -> 0 us
    all_gather x1 -> x0, blocking collectives: 35.7 us -> none  [per_device(): key_group = lax.all_gather(keys_values, 'outer', axis=0, tiled=True)]
  transfers between devices with their start and end apart: 34 -> 35, of which waited for: 34 -> 35; matrix products, arithmetic and copies ran while one was open for 1% -> 2% of each run, Pallas kernels for 0% -> 0%
where the time goes in v1:
time: 1460 us
  waiting for transfers between devices  971 us (67%)
  local copies, waits for them, and re-layouts  240 us (16%)
  matrix products  153 us (10%)
  other arithmetic  69.1 us (5%)
    unnamed x3, waiting for transfers between devices  653 us
    ppermute x32, waiting for transfers between devices, passed_along(): lax.ppermute(value, axis, [(i, (i + by) % devices) for i in range(devices)])  245 us
    gather x16, local copies, waits for them, and re-layouts, key_meta(): key_pos = jnp.take(span_order, span_ids) * half_len + key_ids % half_len  110 us
    gather x16, local copies, waits for them, and re-layouts, key_meta(): return (key_pos, jnp.take(doc_ids, key_pos))  98.5 us
    reduce_scatter x1, waiting for transfers between devices, per_device(): lax.psum_scatter(kv_grads.astype(jnp.bfloat16), 'outer', scatter_dimensio...  66.8 us
    dot_general x32, matrix products, one_block(): jnp.einsum('ihc,jc->hij', query_heads, key_rows, preferred_element_type=j...  43.8 us
    dot_general x32, matrix products, one_block(): jnp.einsum('ihc,jc->hij', grad_heads, value_rows, preferred_element_type=...  41 us
    dot_general x32, matrix products, one_block(): jnp.einsum('hij,jc->ihc', score_grads, key_rows, preferred_element_type=j...  39 us
  transfers between devices with their start and end apart: 35, of which 35 were waited for; matrix products, arithmetic and copies ran while one was open for 2% of the time, Pallas kernels for 0%

profile of v1, /device:TPU:0, one launch (start us, length us, event | category | flops | bytes accessed | tf_op | source)
XLA Modules:
  0.0 1460.5 jit_solution(4468271606501329182)
XLA Ops:
  9.1 7.2 all-to-all-start
  27.3 692.3 %while.64 = (s32[]{:T(128)}, bf16[1024,256]{1,0:T(8,128)(2,1)S(1)}, f32[1024,256]{0,1:T(8,128)}, f32[128,6,128]{0,2,1:T(8,128)S(1)}, s32[]{:T(128)}, /*index=5*/...) while((s32[]{:T(128)}, bf16[1024,256]{1,0:T(8,128)(2,1)S(1)}, ...), condition=%wide.region_3.4_spmd.clone, body=%wide.region_0.3_spmd.clone.sunk | while | flops 507945216 | bytes 26042736 | solution.py:107
  27.4 6.9 gather_fusion
  34.3 6.2 gather_fusion.1
  42.8 10.4 while.65
  56.1 8.9 collective-permute-done.1
  70.7 6.9 gather_fusion
  77.6 6.2 gather_fusion.1
  86.1 10.4 while.65
  97.4 10.9 collective-permute-done.1
  113.9 6.9 gather_fusion
  120.9 6.2 gather_fusion.1
  129.4 10.4 while.65
  140.6 10.9 collective-permute-done.1
  157.2 6.9 gather_fusion
  164.1 6.2 gather_fusion.1
  172.6 10.4 while.65
  183.9 10.9 collective-permute-done.1
  200.5 6.9 gather_fusion
  207.4 6.2 gather_fusion.1
  215.9 10.4 while.65
  227.2 10.9 collective-permute-done.1
  243.8 6.9 gather_fusion
  259.2 10.4 while.65
  270.4 10.9 collective-permute-done.1
  287.0 6.9 gather_fusion
  293.9 6.2 gather_fusion.1
  302.4 10.4 while.65
  313.7 10.9 collective-permute-done.1
  330.3 6.9 gather_fusion
  337.2 6.2 gather_fusion.1
  345.7 10.4 while.65
  357.0 10.9 collective-permute-done.1
  373.6 6.9 gather_fusion
  380.5 6.2 gather_fusion.1
  389.0 10.4 while.65
  400.2 10.9 collective-permute-done.1
  416.8 6.9 gather_fusion
  423.7 6.2 gather_fusion.1
  432.2 10.4 while.65
  443.5 10.9 collective-permute-done.1
  460.1 6.9 gather_fusion
  467.0 6.2 gather_fusion.1
  475.5 10.4 while.65
  486.8 10.9 collective-permute-done.1
  503.4 6.9 gather_fusion
  510.3 6.2 gather_fusion.1
  518.8 10.4 while.65
  530.0 10.9 collective-permute-done.1
  546.6 6.9 gather_fusion
  562.1 10.4 while.65
  573.3 10.9 collective-permute-done.1
  589.9 6.9 gather_fusion
  605.3 10.4 while.65
  616.6 10.9 collective-permute-done.1
  633.2 6.9 gather_fusion
  648.6 10.4 while.65
  659.8 10.9 collective-permute-done.1
  676.4 6.9 gather_fusion
  691.9 10.4 while.65
  703.1 10.9 collective-permute-done.1
  722.0 66.8 %reduce-scatter.5.cloned.1.call-done = bf16[128,256]{1,0:T(8,128)(2,1)} async-done(((bf16[1024,256]{1,0:T(8,128)(2,1)}), bf16[128,256]{1,0:T(8,128)(2,1)}) %reduce-scatter.5.cloned.1.call-update) | async-done | bytes 65552 | tf_op jit(solution)/shard_map/reduce_scatter | solution.py:108
  793.3 6.6 copy.62
  800.7 652.9 %reduce-scatter.7.cloned.1.call-done = f32[48,256]{1,0:T(8,128)} async-done(((f32[6144,256]{1,0:T(8,128)}), f32[48,256]{1,0:T(8,128)}) %reduce-scatter.7.cloned.1.call-update) | async-done | bytes 49168
  (569 shorter events, 358.9 us)
Async XLA Ops:
  7.2 781.6 %copy-start = (bf16[128,6144]{1,0:T(8,128)(2,1)S(1)}, bf16[128,6144]{1,0:T(8,128)(2,1)}, u32[]{:S(2)}) copy-start(bf16[128,6144]{1,0:T(8,128)(2,1)} %param.12) | copy-start | bytes 4718596
  7.2 9.1 copy-start.1
  7.2 9.9 copy-start.4
  7.2 10.0 copy-start.5
  7.2 10.2 copy-start.6
  7.2 11.7 copy-start.2
  9.1 18.2 %copy-start.7 = (f32[6,128]{1,0:T(8,128)S(1)}, f32[6,128]{1,0:T(8,128)}, u32[]{:S(2)}) copy-start(f32[6,128]{1,0:T(8,128)} %param.17) | copy-start | bytes 9220
  9.1 18.2 %all-to-all-start = ((bf16[8,128,256]{2,1,0:T(8,128)(2,1)}), bf16[8,128,256]{2,1,0:T(8,128)(2,1)S(1)}, u32[]{:S(2)}, u32[]{:S(2)}) async-start(bf16[8,128,256]{2,1,0:T(8,128)(2,1)} %stack.2), calls=%async_computation | async-start | bytes 1048576 | tf_op jit(solution)/shard_map/all_to_all | solution.py:87
  16.3 772.5 %reduce-scatter.5.cloned.1.call-start = ((), (), s32[]{:S(2)}) async-start(), calls=%async_computation.3 | async-start | bytes 589824 | tf_op jit(solution)/shard_map/reduce_scatter | solution.py:108
  40.5 2.2 copy-start.3
  54.1 10.9 collective-permute-start.1
  54.1 16.5 %collective-permute-start = (bf16[1024,256]{1,0:T(8,128)(2,1)}, bf16[1024,256]{1,0:T(8,128)(2,1)S(1)}, u32[]{:S(2)}, u32[]{:S(2)}) collective-permute-start(bf16[1024,256]{1,0:T(8,128)(2,1)} %copy.80), channel_id=1, source_target_pairs={{0,8},{8,16},{16,24},{24,32},{32,40},{40,48},{48,56},{56,64},{64,7... | collective-permute-start | bytes 1572872 | tf_op jit(solution)/shard_map/while/body/eval_jaxpr/ppermute | solution.py:9
  83.8 2.2 copy-start.3
  97.4 10.9 collective-permute-start.1
  97.4 16.5 %collective-permute-start = (bf16[1024,256]{1,0:T(8,128)(2,1)}, bf16[1024,256]{1,0:T(8,128)(2,1)S(1)}, u32[]{:S(2)}, u32[]{:S(2)}) collective-permute-start(bf16[1024,256]{1,0:T(8,128)(2,1)} %copy.80), channel_id=1, source_target_pairs={{0,8},{8,16},{16,24},{24,32},{32,40},{40,48},{48,56},{56,64},{64,7... | collective-permute-start | bytes 1572872 | tf_op jit(solution)/shard_map/while/body/eval_jaxpr/ppermute | solution.py:9
  127.0 2.2 copy-start.3
  140.6 10.9 collective-permute-start.1
  140.6 16.5 %collective-permute-start = (bf16[1024,256]{1,0:T(8,128)(2,1)}, bf16[1024,256]{1,0:T(8,128)(2,1)S(1)}, u32[]{:S(2)}, u32[]{:S(2)}) collective-permute-start(bf16[1024,256]{1,0:T(8,128)(2,1)} %copy.80), channel_id=1, source_target_pairs={{0,8},{8,16},{16,24},{24,32},{32,40},{40,48},{48,56},{56,64},{64,7... | collective-permute-start | bytes 1572872 | tf_op jit(solution)/shard_map/while/body/eval_jaxpr/ppermute | solution.py:9
  170.3 2.2 copy-start.3
  183.9 10.9 collective-permute-start.1
  183.9 16.5 %collective-permute-start = (bf16[1024,256]{1,0:T(8,128)(2,1)}, bf16[1024,256]{1,0:T(8,128)(2,1)S(1)}, u32[]{:S(2)}, u32[]{:S(2)}) collective-permute-start(bf16[1024,256]{1,0:T(8,128)(2,1)} %copy.80), channel_id=1, source_target_pairs={{0,8},{8,16},{16,24},{24,32},{32,40},{40,48},{48,56},{56,64},{64,7... | collective-permute-start | bytes 1572872 | tf_op jit(solution)/shard_map/while/body/eval_jaxpr/ppermute | solution.py:9
  213.6 2.2 copy-start.3
  227.2 10.9 collective-permute-start.1
  227.2 16.5 %collective-permute-start = (bf16[1024,256]{1,0:T(8,128)(2,1)}, bf16[1024,256]{1,0:T(8,128)(2,1)S(1)}, u32[]{:S(2)}, u32[]{:S(2)}) collective-permute-start(bf16[1024,256]{1,0:T(8,128)(2,1)} %copy.80), channel_id=1, source_target_pairs={{0,8},{8,16},{16,24},{24,32},{32,40},{40,48},{48,56},{56,64},{64,7... | collective-permute-start | bytes 1572872 | tf_op jit(solution)/shard_map/while/body/eval_jaxpr/ppermute | solution.py:9
  256.8 2.2 copy-start.3
  270.4 10.9 collective-permute-start.1
  270.4 16.5 %collective-permute-start = (bf16[1024,256]{1,0:T(8,128)(2,1)}, bf16[1024,256]{1,0:T(8,128)(2,1)S(1)}, u32[]{:S(2)}, u32[]{:S(2)}) collective-permute-start(bf16[1024,256]{1,0:T(8,128)(2,1)} %copy.80), channel_id=1, source_target_pairs={{0,8},{8,16},{16,24},{24,32},{32,40},{40,48},{48,56},{56,64},{64,7... | collective-permute-start | bytes 1572872 | tf_op jit(solution)/shard_map/while/body/eval_jaxpr/ppermute | solution.py:9
  300.1 2.2 copy-start.3
  313.7 10.9 collective-permute-start.1
  313.7 16.5 %collective-permute-start = (bf16[1024,256]{1,0:T(8,128)(2,1)}, bf16[1024,256]{1,0:T(8,128)(2,1)S(1)}, u32[]{:S(2)}, u32[]{:S(2)}) collective-permute-start(bf16[1024,256]{1,0:T(8,128)(2,1)} %copy.80), channel_id=1, source_target_pairs={{0,8},{8,16},{16,24},{24,32},{32,40},{40,48},{48,56},{56,64},{64,7... | collective-permute-start | bytes 1572872 | tf_op jit(solution)/shard_map/while/body/eval_jaxpr/ppermute | solution.py:9
  343.4 2.2 copy-start.3
  357.0 10.9 collective-permute-start.1
  357.0 16.5 %collective-permute-start = (bf16[1024,256]{1,0:T(8,128)(2,1)}, bf16[1024,256]{1,0:T(8,128)(2,1)S(1)}, u32[]{:S(2)}, u32[]{:S(2)}) collective-permute-start(bf16[1024,256]{1,0:T(8,128)(2,1)} %copy.80), channel_id=1, source_target_pairs={{0,8},{8,16},{16,24},{24,32},{32,40},{40,48},{48,56},{56,64},{64,7... | collective-permute-start | bytes 1572872 | tf_op jit(solution)/shard_map/while/body/eval_jaxpr/ppermute | solution.py:9
  386.6 2.2 copy-start.3
  400.2 10.9 collective-permute-start.1
  400.2 16.5 %collective-permute-start = (bf16[1024,256]{1,0:T(8,128)(2,1)}, bf16[1024,256]{1,0:T(8,128)(2,1)S(1)}, u32[]{:S(2)}, u32[]{:S(2)}) collective-permute-start(bf16[1024,256]{1,0:T(8,128)(2,1)} %copy.80), channel_id=1, source_target_pairs={{0,8},{8,16},{16,24},{24,32},{32,40},{40,48},{48,56},{56,64},{64,7... | collective-permute-start | bytes 1572872 | tf_op jit(solution)/shard_map/while/body/eval_jaxpr/ppermute | solution.py:9
  429.9 2.2 copy-start.3
  443.5 10.9 collective-permute-start.1
  443.5 16.5 %collective-permute-start = (bf16[1024,256]{1,0:T(8,128)(2,1)}, bf16[1024,256]{1,0:T(8,128)(2,1)S(1)}, u32[]{:S(2)}, u32[]{:S(2)}) collective-permute-start(bf16[1024,256]{1,0:T(8,128)(2,1)} %copy.80), channel_id=1, source_target_pairs={{0,8},{8,16},{16,24},{24,32},{32,40},{40,48},{48,56},{56,64},{64,7... | collective-permute-start | bytes 1572872 | tf_op jit(solution)/shard_map/while/body/eval_jaxpr/ppermute | solution.py:9
  473.2 2.2 copy-start.3
  486.8 10.9 collective-permute-start.1
  486.8 16.5 %collective-permute-start = (bf16[1024,256]{1,0:T(8,128)(2,1)}, bf16[1024,256]{1,0:T(8,128)(2,1)S(1)}, u32[]{:S(2)}, u32[]{:S(2)}) collective-permute-start(bf16[1024,256]{1,0:T(8,128)(2,1)} %copy.80), channel_id=1, source_target_pairs={{0,8},{8,16},{16,24},{24,32},{32,40},{40,48},{48,56},{56,64},{64,7... | collective-permute-start | bytes 1572872 | tf_op jit(solution)/shard_map/while/body/eval_jaxpr/ppermute | solution.py:9
  516.4 2.2 copy-start.3
  530.0 10.9 collective-permute-start.1
  530.0 16.5 %collective-permute-start = (bf16[1024,256]{1,0:T(8,128)(2,1)}, bf16[1024,256]{1,0:T(8,128)(2,1)S(1)}, u32[]{:S(2)}, u32[]{:S(2)}) collective-permute-start(bf16[1024,256]{1,0:T(8,128)(2,1)} %copy.80), channel_id=1, source_target_pairs={{0,8},{8,16},{16,24},{24,32},{32,40},{40,48},{48,56},{56,64},{64,7... | collective-permute-start | bytes 1572872 | tf_op jit(solution)/shard_map/while/body/eval_jaxpr/ppermute | solution.py:9
  559.7 2.2 copy-start.3
  573.3 10.9 collective-permute-start.1
  573.3 16.5 %collective-permute-start = (bf16[1024,256]{1,0:T(8,128)(2,1)}, bf16[1024,256]{1,0:T(8,128)(2,1)S(1)}, u32[]{:S(2)}, u32[]{:S(2)}) collective-permute-start(bf16[1024,256]{1,0:T(8,128)(2,1)} %copy.80), channel_id=1, source_target_pairs={{0,8},{8,16},{16,24},{24,32},{32,40},{40,48},{48,56},{56,64},{64,7... | collective-permute-start | bytes 1572872 | tf_op jit(solution)/shard_map/while/body/eval_jaxpr/ppermute | solution.py:9
  603.0 2.2 copy-start.3
  616.6 10.9 collective-permute-start.1
  616.6 16.5 %collective-permute-start = (bf16[1024,256]{1,0:T(8,128)(2,1)}, bf16[1024,256]{1,0:T(8,128)(2,1)S(1)}, u32[]{:S(2)}, u32[]{:S(2)}) collective-permute-start(bf16[1024,256]{1,0:T(8,128)(2,1)} %copy.80), channel_id=1, source_target_pairs={{0,8},{8,16},{16,24},{24,32},{32,40},{40,48},{48,56},{56,64},{64,7... | collective-permute-start | bytes 1572872 | tf_op jit(solution)/shard_map/while/body/eval_jaxpr/ppermute | solution.py:9
  646.2 2.2 copy-start.3
  659.8 10.9 collective-permute-start.1
  659.8 16.5 %collective-permute-start = (bf16[1024,256]{1,0:T(8,128)(2,1)}, bf16[1024,256]{1,0:T(8,128)(2,1)S(1)}, u32[]{:S(2)}, u32[]{:S(2)}) collective-permute-start(bf16[1024,256]{1,0:T(8,128)(2,1)} %copy.80), channel_id=1, source_target_pairs={{0,8},{8,16},{16,24},{24,32},{32,40},{40,48},{48,56},{56,64},{64,7... | collective-permute-start | bytes 1572872 | tf_op jit(solution)/shard_map/while/body/eval_jaxpr/ppermute | solution.py:9
  689.5 2.2 copy-start.3
  703.1 10.9 collective-permute-start.1
  703.1 16.5 %collective-permute-start = (bf16[1024,256]{1,0:T(8,128)(2,1)}, bf16[1024,256]{1,0:T(8,128)(2,1)S(1)}, u32[]{:S(2)}, u32[]{:S(2)}) collective-permute-start(bf16[1024,256]{1,0:T(8,128)(2,1)} %copy.80), channel_id=1, source_target_pairs={{0,8},{8,16},{16,24},{24,32},{32,40},{40,48},{48,56},{56,64},{64,7... | collective-permute-start | bytes 1572872 | tf_op jit(solution)/shard_map/while/body/eval_jaxpr/ppermute | solution.py:9
  721.9 731.7 %reduce-scatter.7.cloned.1.call-start = ((), (), s32[]{:S(2)}) async-start(), calls=%async_computation.4 | async-start | bytes 6340608
Sparse Core Ops, SparseCore 0:
  722.1 66.6 reduce-scatter.4
  800.0 653.6 reduce-scatter.6
